TPU v7x, 32 devices: a whole 2x2x4 slice. The times are simulated.
32 devices in a mesh: dp: 8 (over z, y), tp: 4 (over x, core).
Axes of the slice: x: 2, y: 2, z: 4, core: 2. Of those that a mesh axis runs over, the one named last changes fastest.
Arguments:
- hidden_in: bfloat16 [2, 8192, 1024], P(None, ('dp', 'tp')), may hold values from -6 to 6
- out_grad: bfloat16 [2, 8192, 1024], P(None, ('dp', 'tp')), may hold values from -6 to 6
- domain_ids: int32 [16], replicated, may hold values from 0 to 7
- domain_weights: float32 [8], replicated, may hold values from 0.5 to 2
- gain_attn: float32 [1024], P(('dp', 'tp')), may hold values from 0.1 to 1.9
- gain_mlp: float32 [1024], P(('dp', 'tp')), may hold values from 0.1 to 1.9
- w_query: bfloat16 [1024, 1024], P('dp', 'tp'), may hold values from -0.1875 to 0.1875
- w_kv: bfloat16 [1024, 256], P('dp', 'tp'), may hold values from -0.1875 to 0.1875
- w_out: bfloat16 [1024, 1024], P('tp', 'dp'), may hold values from -0.75 to 0.75
- w_gate: bfloat16 [1024, 2816], P('dp', 'tp'), may hold values from -0.1875 to 0.1875
- w_up: bfloat16 [1024, 2816], P('dp', 'tp'), may hold values from -0.1875 to 0.1875
- w_down: bfloat16 [2816, 1024], P('tp', 'dp'), may hold values from -0.109375 to 0.109375
Outputs:
- block_out: float32 [2, 8192, 1024], P(None, ('dp', 'tp'))
- input_grad: float32 [2, 8192, 1024], P(None, ('dp', 'tp'))
- gain_attn_grad: float32 [1024], P(('dp', 'tp'))
- gain_mlp_grad: float32 [1024], P(('dp', 'tp'))
- w_query_grad: float32 [1024, 1024], P('dp', 'tp')
- w_kv_grad: float32 [1024, 256], P('dp', 'tp')
- w_out_grad: float32 [1024, 1024], P('tp', 'dp')
- w_gate_grad: float32 [1024, 2816], P('dp', 'tp')
- w_up_grad: float32 [1024, 2816], P('dp', 'tp')
- w_down_grad: float32 [2816, 1024], P('tp', 'dp')
All inputs are finite; a program needn't handle non-finite values.
Results may differ from a plain program's by a relative error of at most 0.02.
Values may be sent and summed in bfloat16 or wider, within the bound.
No kernel may reach another device: no remote copies, remote signals or barrier semaphores. Data moves between devices by JAX's collectives and lax.ppermute only.
A program may use at most 192 MiB of HBM per device.

v0:
```python
import jax
import jax.numpy as jnp
from jax import lax
from jax.sharding import PartitionSpec as P

epsilon = 1e-06
neg_large = -1e30


def rope_tables(length, head_size):
    quarter = head_size // 4
    position = jnp.arange(length).astype(jnp.float32)
    frequency = 10000.0 ** (-jnp.arange(quarter).astype(jnp.float32) / quarter)
    angles = position[:, None] * frequency[None, :]
    return (jnp.cos(angles), jnp.sin(angles))


def rotate_half(values, cosine_table, sine_table):
    quarter = cosine_table.shape[-1]
    first_half = values[..., :quarter]
    paired = values[..., quarter : 2 * quarter]
    remainder = values[..., 2 * quarter :]
    return jnp.concatenate(
        [
            first_half * cosine_table - paired * sine_table,
            paired * cosine_table + first_half * sine_table,
            remainder,
        ],
        -1,
    )


def norm_forward(values, scales):
    inverse = lax.rsqrt(jnp.mean(values * values, -1, keepdims=True) + epsilon)
    unit_rows = values * inverse
    return (inverse, unit_rows, unit_rows * scales)


def norm_backward(grad_rows, inverse, unit_rows, scales):
    scaled = grad_rows * scales
    return inverse * (scaled - unit_rows * jnp.mean(scaled * unit_rows, -1, keepdims=True))


def masked_scores(query_block, key_rows, row_start):
    scores = jnp.einsum("tha,ua->htu", query_block, key_rows, preferred_element_type=jnp.float32)
    row_pos = row_start + jnp.arange(query_block.shape[0])
    col_pos = jnp.arange(key_rows.shape[0])
    return jnp.where(col_pos[None, None, :] <= row_pos[None, :, None], scores, neg_large)


def attend_forward(rotated, key_rows, value_rows):
    length = rotated.shape[0]
    block_rows = min(512, length)
    outputs = []
    totals = []
    for row_start in range(0, length, block_rows):
        scores = masked_scores(rotated[row_start : row_start + block_rows], key_rows, row_start)
        row_peak = jnp.max(scores, -1, keepdims=True)
        log_total = row_peak + jnp.log(jnp.sum(jnp.exp(scores - row_peak), -1, keepdims=True))
        probs_low = jnp.exp(scores - log_total).astype(jnp.bfloat16)
        outputs.append(
            jnp.einsum("htu,ua->tha", probs_low, value_rows, preferred_element_type=jnp.float32)
        )
        totals.append(log_total)
    return (jnp.concatenate(outputs, 0), totals)


def attend_backward(rotated, key_rows, value_rows, grad_mixed, totals):
    length = rotated.shape[0]
    block_rows = min(512, length)
    query_grads = []
    key_grad = jnp.zeros(key_rows.shape, jnp.float32)
    value_grad = jnp.zeros(value_rows.shape, jnp.float32)
    for block_idx, row_start in enumerate(range(0, length, block_rows)):
        query_block = rotated[row_start : row_start + block_rows]
        scores = masked_scores(query_block, key_rows, row_start)
        probs = jnp.exp(scores - totals[block_idx])
        probs_low = probs.astype(jnp.bfloat16)
        grad_block = grad_mixed[row_start : row_start + block_rows]
        grad_probs = jnp.einsum(
            "tha,ua->htu", grad_block, value_rows, preferred_element_type=jnp.float32
        )
        inner = jnp.sum(probs * grad_probs, -1, keepdims=True)
        grad_scores = (probs * (grad_probs - inner)).astype(jnp.bfloat16)
        query_grads.append(
            jnp.einsum("htu,ua->tha", grad_scores, key_rows, preferred_element_type=jnp.float32)
        )
        key_grad = key_grad + jnp.einsum(
            "htu,tha->ua", grad_scores, query_block, preferred_element_type=jnp.float32
        )
        value_grad = value_grad + jnp.einsum(
            "htu,tha->ua", probs_low, grad_block, preferred_element_type=jnp.float32
        )
    return (jnp.concatenate(query_grads, 0), key_grad, value_grad)


def local(
    hidden_in,
    out_grad,
    domain_ids,
    domain_weights,
    gain_attn,
    gain_mlp,
    w_query,
    w_kv,
    w_out,
    w_gate,
    w_up,
    w_down,
):
    micro = hidden_in.shape[0]
    n_data = lax.axis_size("dp")
    n_seqs = domain_ids.shape[0]
    head_size = w_kv.shape[1]
    per_group = w_query.shape[1] // head_size
    head_scale = head_size ** (-0.5)
    labels = jnp.arange(domain_weights.shape[0], dtype=jnp.int32)
    one_hot = (domain_ids[:, None] == labels[None, :]).astype(jnp.float32)
    counts = jnp.sum(one_hot, 0)
    gain_one, gain_two = (
        lax.all_gather(gain_attn, ("dp", "tp"), axis=0, tiled=True),
        lax.all_gather(gain_mlp, ("dp", "tp"), axis=0, tiled=True),
    )
    length = hidden_in.shape[1] * lax.axis_size("tp")
    cosine_table, sine_table = rope_tables(length, head_size)
    cos_heads = cosine_table[:, None, :]
    sin_heads = sine_table[:, None, :]
    gain_grad_one = jnp.zeros(gain_one.shape, jnp.float32)
    gain_grad_two = jnp.zeros(gain_two.shape, jnp.float32)
    outputs = []
    input_grads = []
    grad_totals = None
    for micro_idx in range(micro):
        weights_now = (
            lax.all_gather(w_query, "dp", axis=0, tiled=True),
            lax.all_gather(w_kv, "dp", axis=0, tiled=True),
            lax.all_gather(w_out, "dp", axis=1, tiled=True),
            lax.all_gather(w_gate, "dp", axis=0, tiled=True),
            lax.all_gather(w_up, "dp", axis=0, tiled=True),
            lax.all_gather(w_down, "dp", axis=1, tiled=True),
        )
        query_full, kv_full, out_full, gate_full, up_full, down_full = weights_now
        tokens = hidden_in[micro_idx].astype(jnp.float32)
        seq_index = micro_idx * n_data + lax.axis_index("dp")
        domain = lax.dynamic_index_in_dim(domain_ids, seq_index, keepdims=False)
        domain_pick = (labels == domain).astype(jnp.float32)
        factor = jnp.sum(domain_pick * domain_weights) * lax.rsqrt(
            jnp.sum(domain_pick * counts) * counts.shape[0] / n_seqs
        )
        inverse_one, unit_one, normed_one = norm_forward(tokens, gain_one)
        whole_one = lax.all_gather(normed_one.astype(jnp.bfloat16), "tp", axis=0, tiled=True)
        queries = jnp.dot(whole_one, query_full, preferred_element_type=jnp.float32).reshape(
            length, per_group, head_size
        )
        rotated = (rotate_half(queries, cos_heads, sin_heads) * head_scale).astype(jnp.bfloat16)
        kv_state = jnp.dot(whole_one, kv_full, preferred_element_type=jnp.float32)
        key_rows = rotate_half(kv_state, cosine_table, sine_table).astype(jnp.bfloat16)
        value_rows = kv_state.astype(jnp.bfloat16)
        mixed_out, totals = attend_forward(rotated, key_rows, value_rows)
        mixed_low = mixed_out.astype(jnp.bfloat16).reshape(length, per_group * head_size)
        attn_sum = lax.psum_scatter(
            jnp.dot(mixed_low, out_full, preferred_element_type=jnp.float32).astype(jnp.bfloat16),
            "tp",
            scatter_dimension=0,
            tiled=True,
        ).astype(jnp.float32)
        residual = tokens + attn_sum
        inverse_two, unit_two, normed_two = norm_forward(residual, gain_two)
        whole_two = lax.all_gather(normed_two.astype(jnp.bfloat16), "tp", axis=0, tiled=True)
        gate_val = jnp.dot(whole_two, gate_full, preferred_element_type=jnp.float32)
        up_val = jnp.dot(whole_two, up_full, preferred_element_type=jnp.float32)
        sigmoid_val = jax.nn.sigmoid(gate_val)
        silu_val = gate_val * sigmoid_val
        hidden_low = (silu_val * up_val).astype(jnp.bfloat16)
        branch = lax.psum_scatter(
            jnp.dot(hidden_low, down_full, preferred_element_type=jnp.float32).astype(jnp.bfloat16),
            "tp",
            scatter_dimension=0,
            tiled=True,
        ).astype(jnp.float32)
        outputs.append(residual + branch)
        weights_later = (
            lax.all_gather(w_query, "dp", axis=0, tiled=True),
            lax.all_gather(w_kv, "dp", axis=0, tiled=True),
            lax.all_gather(w_out, "dp", axis=1, tiled=True),
            lax.all_gather(w_gate, "dp", axis=0, tiled=True),
            lax.all_gather(w_up, "dp", axis=0, tiled=True),
            lax.all_gather(w_down, "dp", axis=1, tiled=True),
        )
        query_back, kv_back, out_back, gate_back, up_back, down_back = weights_later
        grad_out = out_grad[micro_idx].astype(jnp.float32) * factor
        grad_rows = lax.all_gather(grad_out.astype(jnp.bfloat16), "tp", axis=0, tiled=True)
        grad_hidden = jnp.einsum(
            "td,fd->tf", grad_rows, down_back, preferred_element_type=jnp.float32
        )
        grad_gate = (
            grad_hidden * up_val * sigmoid_val * (1.0 + gate_val * (1.0 - sigmoid_val))
        ).astype(jnp.bfloat16)
        grad_up = (grad_hidden * silu_val).astype(jnp.bfloat16)
        down_grad = jnp.einsum(
            "tf,td->fd", hidden_low, grad_rows, preferred_element_type=jnp.float32
        )
        gate_grad = jnp.einsum(
            "td,tf->df", whole_two, grad_gate, preferred_element_type=jnp.float32
        )
        up_grad = jnp.einsum("td,tf->df", whole_two, grad_up, preferred_element_type=jnp.float32)
        normed_two_part = jnp.einsum(
            "tf,df->td", grad_gate, gate_back, preferred_element_type=jnp.float32
        ) + jnp.einsum("tf,df->td", grad_up, up_back, preferred_element_type=jnp.float32)
        grad_normed_two = lax.psum_scatter(
            normed_two_part.astype(jnp.bfloat16), "tp", scatter_dimension=0, tiled=True
        ).astype(jnp.float32)
        gain_grad_two = gain_grad_two + jnp.sum(grad_normed_two * unit_two, 0)
        grad_residual = grad_out + norm_backward(grad_normed_two, inverse_two, unit_two, gain_two)
        grad_attn = lax.all_gather(grad_residual.astype(jnp.bfloat16), "tp", axis=0, tiled=True)
        out_grad_part = jnp.einsum(
            "tq,td->qd", mixed_low, grad_attn, preferred_element_type=jnp.float32
        )
        grad_mixed = jnp.einsum(
            "td,qd->tq", grad_attn, out_back, preferred_element_type=jnp.float32
        )
        grad_mixed = grad_mixed.astype(jnp.bfloat16).reshape(length, per_group, head_size)
        grad_rotated, key_grad, value_grad = attend_backward(
            rotated, key_rows, value_rows, grad_mixed, totals
        )
        grad_query = (rotate_half(grad_rotated, cos_heads, -sin_heads) * head_scale).astype(
            jnp.bfloat16
        )
        grad_query = grad_query.reshape(length, per_group * head_size)
        grad_kv = (value_grad + rotate_half(key_grad, cosine_table, -sine_table)).astype(
            jnp.bfloat16
        )
        query_grad = jnp.einsum(
            "td,tq->dq", whole_one, grad_query, preferred_element_type=jnp.float32
        )
        kv_grad = jnp.einsum("td,tk->dk", whole_one, grad_kv, preferred_element_type=jnp.float32)
        normed_one_part = jnp.einsum(
            "tq,dq->td", grad_query, query_back, preferred_element_type=jnp.float32
        ) + jnp.einsum("tk,dk->td", grad_kv, kv_back, preferred_element_type=jnp.float32)
        grad_normed_one = lax.psum_scatter(
            normed_one_part.astype(jnp.bfloat16), "tp", scatter_dimension=0, tiled=True
        ).astype(jnp.float32)
        gain_grad_one = gain_grad_one + jnp.sum(grad_normed_one * unit_one, 0)
        input_grads.append(
            grad_residual + norm_backward(grad_normed_one, inverse_one, unit_one, gain_one)
        )
        grads_now = (query_grad, kv_grad, out_grad_part, gate_grad, up_grad, down_grad)
        if micro_idx == 0:
            grad_totals = grads_now
        else:
            grad_totals = tuple((total + grad for total, grad in zip(grad_totals, grads_now)))
    query_total, kv_total, out_total, gate_total, up_total, down_total = grad_totals
    final_grads = (
        lax.psum_scatter(query_total, "dp", scatter_dimension=0, tiled=True),
        lax.psum_scatter(kv_total, "dp", scatter_dimension=0, tiled=True),
        lax.psum_scatter(out_total, "dp", scatter_dimension=1, tiled=True),
        lax.psum_scatter(gate_total, "dp", scatter_dimension=0, tiled=True),
        lax.psum_scatter(up_total, "dp", scatter_dimension=0, tiled=True),
        lax.psum_scatter(down_total, "dp", scatter_dimension=1, tiled=True),
    )
    gain_one_shard, gain_two_shard = (
        lax.psum_scatter(gain_grad_one, ("dp", "tp"), scatter_dimension=0, tiled=True),
        lax.psum_scatter(gain_grad_two, ("dp", "tp"), scatter_dimension=0, tiled=True),
    )
    return (
        jnp.stack(outputs, 0),
        jnp.stack(input_grads, 0),
        gain_one_shard,
        gain_two_shard,
        final_grads[0],
        final_grads[1],
        final_grads[2],
        final_grads[3],
        final_grads[4],
        final_grads[5],
    )


def solution(mesh):
    return jax.shard_map(
        local,
        mesh=mesh,
        in_specs=(
            P(None, ("dp", "tp"), None),
            P(None, ("dp", "tp"), None),
            P(),
            P(),
            P(("dp", "tp")),
            P(("dp", "tp")),
            P("dp", "tp"),
            P("dp", "tp"),
            P("tp", "dp"),
            P("dp", "tp"),
            P("dp", "tp"),
            P("tp", "dp"),
        ),
        out_specs=(
            P(None, ("dp", "tp"), None),
            P(None, ("dp", "tp"), None),
            P(("dp", "tp")),
            P(("dp", "tp")),
            P("dp", "tp"),
            P("dp", "tp"),
            P("tp", "dp"),
            P("dp", "tp"),
            P("dp", "tp"),
            P("tp", "dp"),
        ),
        check_vma=False,
    )
```

profile of v0, /device:TPU:0, one launch (start us, length us, event | category | flops | bytes accessed | tf_op | source)
XLA Modules:
  0.0 1190.9 jit_solution(2056927915261358699)
XLA Ops:
  11.3 42.1 %all-reduce.5 = (f32[1024]{0:T(1024)S(1)}, f32[1024]{0:T(1024)S(1)}) all-reduce(f32[1024]{0:T(1024)S(1)} %dynamic-update-slice, f32[1024]{0:T(1024)S(1)} %dynamic-update-slice.1), channel_id=1, replica_groups=mesh['dp'=8,'tp'=4] {'dp','tp'}, use_global_device_ids=true, to_apply=%add | all-reduce | flops 2048 | bytes 16384
  53.4 2.5 fusion.58
  56.7 26.1 %all_gather.68 = bf16[1024,64]{0,1:T(8,128)(2,1)S(1)} all-gather(bf16[128,64]{0,1:T(8,128)(2,1)S(1)} %copy-done.81), channel_id=1, replica_groups=mesh['dp'=8,'tp'=4] {'dp'}, dimensions={0}, use_global_device_ids=true | all-gather | bytes 147456 | tf_op jit(solution)/shard_map/all_gather | solution.py:136
  83.0 33.3 %all_gather.69 = bf16[1024,256]{1,0:T(8,128)(2,1)} all-gather(bf16[128,256]{1,0:T(8,128)(2,1)S(1)} %copy-done.67), channel_id=1, replica_groups=mesh['dp'=8,'tp'=4] {'dp'}, dimensions={0}, use_global_device_ids=true | all-gather | bytes 589824 | tf_op jit(solution)/shard_map/all_gather | solution.py:135
  116.4 28.1 %all_gather.70 = bf16[256,1024]{1,0:T(8,128)(2,1)} all-gather(bf16[256,128]{1,0:T(8,128)(2,1)S(1)} %copy-done.68), channel_id=1, replica_groups=mesh['dp'=8,'tp'=4] {'dp'}, dimensions={1}, use_global_device_ids=true | all-gather | bytes 589824 | tf_op jit(solution)/shard_map/all_gather | solution.py:137
  144.9 3.2 fusion.160
  156.9 6.0 exponential_reduce_fusion.3
  165.4 5.0 exponential_reduce_fusion.2
  175.7 5.1 exponential_reduce_fusion.1
  183.4 5.5 convolution_convert_fusion.7
  193.9 13.0 %reduce-scatter.15.cloned.1.call-done = bf16[256,1024]{1,0:T(8,128)(2,1)} async-done(((bf16[1024,1024]{1,0:T(8,128)(2,1)}), bf16[256,1024]{1,0:T(8,128)(2,1)}) %reduce-scatter.15.cloned.1.call-update) | async-done | bytes 524304 | tf_op jit(solution)/shard_map/reduce_scatter | solution.py:161
  206.9 34.6 %reduce-scatter.19.cloned.1.call-done = bf16[256,1024]{1,0:T(8,128)(2,1)} async-done(((bf16[1024,1024]{1,0:T(8,128)(2,1)}), bf16[256,1024]{1,0:T(8,128)(2,1)}) %reduce-scatter.19.cloned.1.call-update) | async-done | bytes 524304 | tf_op jit(solution)/shard_map/reduce_scatter | solution.py:161
  243.1 2.6 multiply_convert_fusion.7
  255.6 12.7 %all-gather.24.cloned.1.call-done = bf16[1024,1024]{1,0:T(8,128)(2,1)} async-done(((bf16[256,1024]{1,0:T(8,128)(2,1)}), bf16[1024,1024]{1,0:T(8,128)(2,1)}) %all-gather.24.cloned.1.call-update) | async-done | bytes 2097168 | tf_op jit(solution)/shard_map/all_gather | solution.py:169
  268.3 5.2 fusion.166
  273.5 39.8 %all-gather.16.cloned.1.call-done = bf16[1024,704]{0,1:T(8,128)(2,1)} async-done(((bf16[128,704]{0,1:T(8,128)(2,1)}), bf16[1024,704]{0,1:T(8,128)(2,1)}) %all-gather.16.cloned.1.call-update) | async-done | bytes 1441808 | tf_op jit(solution)/shard_map/all_gather | solution.py:138
  313.3 5.3 fusion.165
  318.6 38.1 %all-gather.20.cloned.1.call-done = bf16[704,1024]{1,0:T(8,128)(2,1)} async-done(((bf16[704,128]{1,0:T(8,128)(2,1)}), bf16[704,1024]{1,0:T(8,128)(2,1)}) %all-gather.20.cloned.1.call-update) | async-done | bytes 1441808 | tf_op jit(solution)/shard_map/all_gather | solution.py:140
  356.8 22.3 %all-gather.30.cloned.1.call-done = bf16[1024,1024]{1,0:T(8,128)(2,1)} async-done(((bf16[256,1024]{1,0:T(8,128)(2,1)}), bf16[1024,1024]{1,0:T(8,128)(2,1)}) %all-gather.30.cloned.1.call-update) | async-done | bytes 2097168 | tf_op jit(solution)/shard_map/all_gather | solution.py:192
  379.0 7.7 multiply_convert_fusion
  389.1 3.2 add_convert_fusion.1
  392.6 11.1 all-gather.14.cloned.1.call-done
  403.7 5.4 fusion.163
  409.1 3.3 fusion.162
  412.4 23.2 %all-gather.26.cloned.1.call-done = bf16[1024,1024]{1,0:T(8,128)(2,1)} async-done(((bf16[256,1024]{1,0:T(8,128)(2,1)}), bf16[1024,1024]{1,0:T(8,128)(2,1)}) %all-gather.26.cloned.1.call-update) | async-done | bytes 2097168 | tf_op jit(solution)/shard_map/all_gather | solution.py:192
  435.6 7.7 multiply_convert_fusion.2
  445.7 3.2 add_convert_fusion.3
  449.0 5.0 convolution_convert_fusion.2
  454.3 26.2 %reduce-scatter.23.cloned.1.call-done = bf16[256,1024]{1,0:T(8,128)(2,1)} async-done(((bf16[1024,1024]{1,0:T(8,128)(2,1)}), bf16[256,1024]{1,0:T(8,128)(2,1)}) %reduce-scatter.23.cloned.1.call-update) | async-done | bytes 524304 | tf_op jit(solution)/shard_map/reduce_scatter | solution.py:210
  480.5 2.7 fusion.56
  483.2 31.3 %reduce-scatter.21.cloned.1.call-done = bf16[256,1024]{1,0:T(8,128)(2,1)} async-done(((bf16[1024,1024]{1,0:T(8,128)(2,1)}), bf16[256,1024]{1,0:T(8,128)(2,1)}) %reduce-scatter.21.cloned.1.call-update) | async-done | bytes 524304 | tf_op jit(solution)/shard_map/reduce_scatter | solution.py:175
  514.5 3.8 fusion.154
  518.9 21.9 %all-gather.32.cloned.1.call-done = bf16[1024,1024]{1,0:T(8,128)(2,1)} async-done(((bf16[256,1024]{1,0:T(8,128)(2,1)}), bf16[1024,1024]{1,0:T(8,128)(2,1)}) %all-gather.32.cloned.1.call-update) | async-done | bytes 2097168 | tf_op jit(solution)/shard_map/all_gather | solution.py:215
  540.8 2.6 convolution_convert_fusion.4
  544.1 4.6 fusion.99
  548.7 2.7 convolution_bitcast_fusion.7
  551.4 13.9 %all-gather.28.cloned.1.call-done = bf16[1024,1024]{1,0:T(8,128)(2,1)} async-done(((bf16[256,1024]{1,0:T(8,128)(2,1)}), bf16[1024,1024]{1,0:T(8,128)(2,1)}) %all-gather.28.cloned.1.call-update) | async-done | bytes 2097168 | tf_op jit(solution)/shard_map/all_gather | solution.py:215
  568.5 14.1 %fusion.9 = (f32[4,512]{1,0:T(4,128)S(1)}, f32[4,512]{1,0:T(4,128)S(1)}, f32[1024,512,4]{1,0,2:T(8,128)}) fusion(f32[1024,512,4]{1,0,2:T(8,128)} %copy-done.1, f32[4,512]{1,0:T(4,128)S(1)} %log_add_fusion.3, pred[512,1024]{0,1:T(8,128)(4,1)S(1)} %iota_compare_fusion.1, f32[1024,512,4]{1,0,2:T(8,128)} %fusion.99, f32[4,512]{1,0:T(4,128)S(1)} %log_add_fusion.1, ...), kind=kOutput, calls=%fused_computation.17 | convolution fusion | flops 285208576 | bytes 34504704 | tf_op jit(solution)/shard_map/tha,ua->htu/dot_general | solution.py:80
  582.6 14.7 %fusion.11 = (bf16[4,512,1024]{1,2,0:T(8,128)(2,1)}, bf16[4,512,1024]{1,2,0:T(8,128)(2,1)S(1)}) fusion(f32[1024,512,4]{1,0,2:T(8,128)} %get-tuple-element.108, f32[1024,512,4]{1,0,2:T(8,128)} %copy-done.1, f32[4,512]{1,0:T(4,128)S(1)} %get-tuple-element.26, f32[4,512]{1,0:T(4,128)S(1)} %log_add_fusion.3, pred[512,1024]{0,1:T(8,128)(4,1)S(1)} %iota_compare_fusion.1, ...), kind=kLoop, calls=%fused_computation.19 | loop fusion | flops 20971520 | bytes 42500096 | tf_op jit(solution)/shard_map/convert_element_type | solution.py:84
  597.4 5.8 convolution_bitcast_fusion.9
  605.6 4.3 convolution_bitcast_fusion.1
  609.9 4.5 fusion.97
  614.5 8.8 fusion.6
  623.3 14.8 %fusion.8 = (bf16[4,512,1024]{1,2,0:T(8,128)(2,1)S(1)}, bf16[4,512,1024]{1,2,0:T(8,128)(2,1)}) fusion(f32[1024,512,4]{1,0,2:T(8,128)} %get-tuple-element.107, f32[1024,512,4]{1,0,2:T(8,128)} %copy-done, f32[4,512]{1,0:T(4,128)S(1)} %get-tuple-element.28, f32[4,512]{1,0:T(4,128)S(1)} %log_add_fusion.2, pred[512,1024]{0,1:T(8,128)(4,1)S(1)} %iota_compare_fusion, ...), kind=kLoop, calls=%fused_computation.14 | loop fusion | flops 20971520 | bytes 42500096 | tf_op jit(solution)/shard_map/convert_element_type | solution.py:84
  638.2 3.2 convolution_bitcast_fusion
  658.1 5.9 convolution_bitcast_fusion.11
  668.4 4.5 convolution_convert_fusion.3
  673.0 3.8 fusion.172
  676.9 3.2 convolution_add_fusion.2
  680.2 3.9 fusion.175
  684.1 3.3 convolution_add_fusion
  687.5 3.8 fusion.174
  691.3 3.3 convolution_add_fusion.1
  699.1 2.5 fusion.84
  703.8 2.5 fusion.171
  708.2 12.8 %reduce-scatter.25.cloned.1.call-done = bf16[256,1024]{1,0:T(8,128)(2,1)} async-done(((bf16[1024,1024]{1,0:T(8,128)(2,1)}), bf16[256,1024]{1,0:T(8,128)(2,1)}) %reduce-scatter.25.cloned.1.call-update) | async-done | bytes 524304 | tf_op jit(solution)/shard_map/reduce_scatter | solution.py:240
  723.0 39.5 %all-reduce.4 = (f32[1024]{0:T(1024)S(1)}, f32[1024]{0:T(1024)S(1)}) all-reduce(f32[1024]{0:T(1024)S(1)} %add.272, f32[1024]{0:T(1024)S(1)} %add.273), channel_id=10, replica_groups=mesh['dp'=8,'tp'=4] {'dp','tp'}, use_global_device_ids=true, to_apply=%region_35.36.clone | all-reduce | flops 2048 | bytes 16384
  763.6 2.9 fusion.46
  771.9 59.8 %reduce-scatter.41.cloned.1.call-done = f32[704,128]{1,0:T(8,128)} async-done(((f32[704,1024]{1,0:T(8,128)}), f32[704,128]{1,0:T(8,128)}) %reduce-scatter.41.cloned.1.call-update) | async-done | bytes 360464 | tf_op jit(solution)/shard_map/reduce_scatter | solution.py:259
  831.7 76.1 %reduce-scatter.39.cloned.1.call-done = f32[128,704]{0,1:T(8,128)} async-done(((f32[1024,704]{0,1:T(8,128)}), f32[128,704]{0,1:T(8,128)}) %reduce-scatter.39.cloned.1.call-update) | async-done | bytes 360464 | tf_op jit(solution)/shard_map/reduce_scatter | solution.py:258
  907.8 76.1 %reduce-scatter.37.cloned.1.call-done = f32[128,704]{0,1:T(8,128)} async-done(((f32[1024,704]{0,1:T(8,128)}), f32[128,704]{0,1:T(8,128)}) %reduce-scatter.37.cloned.1.call-update) | async-done | bytes 360464 | tf_op jit(solution)/shard_map/reduce_scatter | solution.py:257
  983.9 65.0 %reduce-scatter.33.cloned.1.call-done = f32[128,64]{0,1:T(8,128)} async-done(((f32[1024,64]{0,1:T(8,128)}), f32[128,64]{0,1:T(8,128)}) %reduce-scatter.33.cloned.1.call-update) | async-done | bytes 32784 | tf_op jit(solution)/shard_map/reduce_scatter | solution.py:255
  1048.9 67.2 %reduce-scatter.35.cloned.1.call-done = f32[256,128]{1,0:T(8,128)} async-done(((f32[256,1024]{1,0:T(8,128)}), f32[256,128]{1,0:T(8,128)}) %reduce-scatter.35.cloned.1.call-update) | async-done | bytes 131088 | tf_op jit(solution)/shard_map/reduce_scatter | solution.py:256
  1116.0 67.0 %reduce-scatter.31.cloned.1.call-done = f32[128,256]{1,0:T(8,128)} async-done(((f32[1024,256]{1,0:T(8,128)}), f32[128,256]{1,0:T(8,128)}) %reduce-scatter.31.cloned.1.call-update) | async-done | bytes 131088 | tf_op jit(solution)/shard_map/reduce_scatter | solution.py:254
  (378 shorter events, 87.2 us)
Async XLA Ops:
  8.0 48.7 %copy-start.81 = (bf16[128,64]{0,1:T(8,128)(2,1)S(1)}, bf16[128,64]{0,1:T(8,128)(2,1)}, u32[]{:S(2)}) copy-start(bf16[128,64]{0,1:T(8,128)(2,1)} %param.19) | copy-start | bytes 49156
  8.0 75.0 %copy-start.67 = (bf16[128,256]{1,0:T(8,128)(2,1)S(1)}, bf16[128,256]{1,0:T(8,128)(2,1)}, u32[]{:S(2)}) copy-start(bf16[128,256]{1,0:T(8,128)(2,1)} %param.18) | copy-start | bytes 196612
  8.0 108.3 %copy-start.68 = (bf16[256,128]{1,0:T(8,128)(2,1)S(1)}, bf16[256,128]{1,0:T(8,128)(2,1)}, u32[]{:S(2)}) copy-start(bf16[256,128]{1,0:T(8,128)(2,1)} %param.20) | copy-start | bytes 196612
  8.0 136.9 %all-gather.22.cloned.1.call-start = ((), (), s32[]{:S(2)}) async-start(), calls=%async_computation.21 | async-start | bytes 2621440 | tf_op jit(solution)/shard_map/all_gather | solution.py:151
  9.6 135.3 %copy-start.75 = (f32[256]{0:T(256)}, f32[256]{0:T(256)S(1)}, u32[]{:S(2)}) copy-start(f32[256]{0:T(256)S(1)} %add_rsqrt_fusion.3) | copy-start | bytes 3076
  9.6 135.3 %copy-start.77 = (f32[256]{0:T(256)}, f32[256]{0:T(256)S(1)}, u32[]{:S(2)}) copy-start(f32[256]{0:T(256)S(1)} %add_rsqrt_fusion.1) | copy-start | bytes 3076
  53.4 91.5 %copy-start.65 = (f32[1024]{0:T(1024)}, f32[1024]{0:T(1024)S(1)}, u32[]{:S(2)}) copy-start(f32[1024]{0:T(1024)S(1)} %get-tuple-element.40) | copy-start | bytes 12292
  55.9 92.2 %all-gather.12.cloned.1.call-start = ((), (), s32[]{:S(2)}) async-start(), calls=%async_computation.14 | async-start | bytes 2621440 | tf_op jit(solution)/shard_map/all_gather | solution.py:151
  56.6 150.2 %reduce-scatter.15.cloned.1.call-start = ((), (), s32[]{:S(2)}) async-start(), calls=%async_computation.15 | async-start | bytes 2621440 | tf_op jit(solution)/shard_map/reduce_scatter | solution.py:161
  82.8 67.7 %copy-start.33 = (bf16[1024,64]{0,1:T(8,128)(2,1)}, bf16[1024,64]{0,1:T(8,128)(2,1)S(1)}, u32[]{:S(2)}) copy-start(bf16[1024,64]{0,1:T(8,128)(2,1)S(1)} %all_gather.68) | copy-start | bytes 393220
  82.8 70.2 %copy-start.87 = (f32[16]{0:T(128)}, f32[16]{0:T(128)S(1)}, u32[]{:S(2)}) copy-start(f32[16]{0:T(128)S(1)} %multiply_power_fusion) | copy-start | bytes 196
  82.9 70.2 %copy-start.71 = (f32[1024]{0:T(1024)}, f32[1024]{0:T(1024)S(1)}, u32[]{:S(2)}) copy-start(f32[1024]{0:T(1024)S(1)} %iota_convert_fusion) | copy-start | bytes 12292
  150.6 19.8 %copy-start.38 = (bf16[1024,64]{0,1:T(8,128)(2,1)}, bf16[1024,64]{0,1:T(8,128)(2,1)S(1)}, u32[]{:S(2)}) copy-start(bf16[1024,64]{0,1:T(8,128)(2,1)S(1)} %get-tuple-element.97) | copy-start | bytes 393220
  153.4 11.9 %copy-start.55 = (bf16[1024,16]{0,1:T(8,128)(2,1)}, bf16[1024,16]{0,1:T(8,128)(2,1)S(1)}, u32[]{:S(2)}) copy-start(bf16[1024,16]{0,1:T(8,128)(2,1)S(1)} %get-tuple-element.92) | copy-start | bytes 98308
  153.4 11.9 %copy-start.57 = (bf16[1024,16]{0,1:T(8,128)(2,1)}, bf16[1024,16]{0,1:T(8,128)(2,1)S(1)}, u32[]{:S(2)}) copy-start(bf16[1024,16]{0,1:T(8,128)(2,1)S(1)} %get-tuple-element.93) | copy-start | bytes 98308
  153.9 11.5 copy-start.18
  155.4 15.0 %copy-start = (f32[1024,512,4]{1,0,2:T(8,128)}, f32[1024,512,4]{1,0,2:T(8,128)S(1)}, u32[]{:S(2)}) copy-start(f32[1024,512,4]{1,0,2:T(8,128)S(1)} %get-tuple-element.100) | copy-start | bytes 25165828
  170.4 452.9 %copy-start.61 = (f32[4,512]{1,0:T(4,128)}, f32[4,512]{1,0:T(4,128)S(1)}, u32[]{:S(2)}) copy-start(f32[4,512]{1,0:T(4,128)S(1)} %log_add_fusion.2) | copy-start | bytes 24580
  175.4 66.1 %reduce-scatter.19.cloned.1.call-start = ((), (), s32[]{:S(2)}) async-start(), calls=%async_computation.22 | async-start | bytes 2621440 | tf_op jit(solution)/shard_map/reduce_scatter | solution.py:161
  183.4 440.0 %copy-start.63 = (f32[4,512]{1,0:T(4,128)}, f32[4,512]{1,0:T(4,128)S(1)}, u32[]{:S(2)}) copy-start(f32[4,512]{1,0:T(4,128)S(1)} %log_add_fusion) | copy-start | bytes 24580
  191.1 50.4 %copy-start.3 = (bf16[2,256,1024]{2,1,0:T(8,128)(2,1)S(1)}, bf16[2,256,1024]{2,1,0:T(8,128)(2,1)}, u32[]{:S(2)}) copy-start(bf16[2,256,1024]{2,1,0:T(8,128)(2,1)} %param.12) | copy-start | bytes 3145732
  193.2 62.4 %all-gather.18.cloned.1.call-start = ((), (), s32[]{:S(2)}) async-start(), calls=%async_computation.18 | async-start | bytes 1622016 | tf_op jit(solution)/shard_map/all_gather | solution.py:139
  193.8 53.3 %copy-start.86 = (s32[16]{0:T(128)S(1)}, s32[16]{0:T(128)}, u32[]{:S(2)}) copy-start(s32[16]{0:T(128)} %param.14) | copy-start | bytes 196
  193.8 54.0 %copy-start.89 = (f32[8]{0:T(128)S(1)}, f32[8]{0:T(128)}, u32[]{:S(2)}) copy-start(f32[8]{0:T(128)} %param.15) | copy-start | bytes 100
  193.8 58.7 %copy-start.16 = (bf16[2,256,1024]{2,1,0:T(8,128)(2,1)S(1)}, bf16[2,256,1024]{2,1,0:T(8,128)(2,1)}, u32[]{:S(2)}) copy-start(bf16[2,256,1024]{2,1,0:T(8,128)(2,1)} %param.13) | copy-start | bytes 3145732
  193.8 74.4 %all-gather.24.cloned.1.call-start = ((), (), s32[]{:S(2)}) async-start(), calls=%async_computation.23 | async-start | bytes 2621440 | tf_op jit(solution)/shard_map/all_gather | solution.py:169
  243.1 271.3 %copy-start.73 = (f32[256]{0:T(256)}, f32[256]{0:T(256)S(1)}, u32[]{:S(2)}) copy-start(f32[256]{0:T(256)S(1)} %add_rsqrt_fusion) | copy-start | bytes 3076
  245.7 67.6 %all-gather.16.cloned.1.call-start = ((), (), s32[]{:S(2)}) async-start(), calls=%async_computation.17 | async-start | bytes 1622016 | tf_op jit(solution)/shard_map/all_gather | solution.py:138
  246.3 110.5 %all-gather.20.cloned.1.call-start = ((), (), s32[]{:S(2)}) async-start(), calls=%async_computation.19 | async-start | bytes 1622016 | tf_op jit(solution)/shard_map/all_gather | solution.py:140
  247.0 132.0 %all-gather.30.cloned.1.call-start = ((), (), s32[]{:S(2)}) async-start(), calls=%async_computation.29 | async-start | bytes 2621440 | tf_op jit(solution)/shard_map/all_gather | solution.py:192
  253.7 150.0 %all-gather.14.cloned.1.call-start = ((), (), s32[]{:S(2)}) async-start(), calls=%async_computation.16 | async-start | bytes 2621440 | tf_op jit(solution)/shard_map/all_gather | solution.py:169
  254.5 181.2 %all-gather.26.cloned.1.call-start = ((), (), s32[]{:S(2)}) async-start(), calls=%async_computation.25 | async-start | bytes 2621440 | tf_op jit(solution)/shard_map/all_gather | solution.py:192
  255.1 199.3 %reduce-scatter.27.cloned.1.call-start = ((), (), s32[]{:S(2)}) async-start(), calls=%async_computation.30 | async-start | bytes 2621440 | tf_op jit(solution)/shard_map/reduce_scatter | solution.py:210
  392.3 88.2 %reduce-scatter.23.cloned.1.call-start = ((), (), s32[]{:S(2)}) async-start(), calls=%async_computation.26 | async-start | bytes 2621440 | tf_op jit(solution)/shard_map/reduce_scatter | solution.py:210
  448.9 65.5 %reduce-scatter.21.cloned.1.call-start = ((), (), s32[]{:S(2)}) async-start(), calls=%async_computation.24 | async-start | bytes 2621440 | tf_op jit(solution)/shard_map/reduce_scatter | solution.py:175
  449.0 31.5 %copy-start.12 = (bf16[256,1024]{1,0:T(8,128)(2,1)S(1)}, bf16[256,1024]{1,0:T(8,128)(2,1)}, u32[]{:S(2)}) copy-start(bf16[256,1024]{1,0:T(8,128)(2,1)} %reduce-scatter.15.cloned.1.call-done) | copy-start | bytes 1572868
  449.0 31.5 %copy-start.14 = (bf16[256,1024]{1,0:T(8,128)(2,1)S(1)}, bf16[256,1024]{1,0:T(8,128)(2,1)}, u32[]{:S(2)}) copy-start(bf16[256,1024]{1,0:T(8,128)(2,1)} %reduce-scatter.19.cloned.1.call-done) | copy-start | bytes 1572868
  454.1 86.8 %all-gather.32.cloned.1.call-start = ((), (), s32[]{:S(2)}) async-start(), calls=%async_computation.31 | async-start | bytes 2621440 | tf_op jit(solution)/shard_map/all_gather | solution.py:215
  483.2 35.1 %copy-start.82 = (f32[256]{0:T(256)}, f32[256]{0:T(256)S(1)}, u32[]{:S(2)}) copy-start(f32[256]{0:T(256)S(1)} %broadcast_multiply_fusion.3) | copy-start | bytes 3076
  483.2 35.1 %copy-start.84 = (f32[256]{0:T(256)}, f32[256]{0:T(256)S(1)}, u32[]{:S(2)}) copy-start(f32[256]{0:T(256)S(1)} %broadcast_multiply_fusion.1) | copy-start | bytes 3076
  518.3 47.1 %all-gather.28.cloned.1.call-start = ((), (), s32[]{:S(2)}) async-start(), calls=%async_computation.27 | async-start | bytes 2621440 | tf_op jit(solution)/shard_map/all_gather | solution.py:215
  518.9 189.4 %reduce-scatter.29.cloned.1.call-start = ((), (), s32[]{:S(2)}) async-start(), calls=%async_computation.32 | async-start | bytes 2621440 | tf_op jit(solution)/shard_map/reduce_scatter | solution.py:240
  548.7 16.7 %copy-start.25 = (bf16[256,1024]{1,0:T(8,128)(2,1)S(1)}, bf16[256,1024]{1,0:T(8,128)(2,1)}, u32[]{:S(2)}) copy-start(bf16[256,1024]{1,0:T(8,128)(2,1)} %all_gather.70) | copy-start | bytes 1572868
  551.4 17.0 %copy-start.39 = (bf16[1024,64]{0,1:T(8,128)(2,1)S(1)}, bf16[1024,64]{0,1:T(8,128)(2,1)}, u32[]{:S(2)}) copy-start(bf16[1024,64]{0,1:T(8,128)(2,1)} %copy-done.38) | copy-start | bytes 393220
  568.5 14.1 %copy-start.44 = (bf16[512,256]{0,1:T(8,128)(2,1)}, bf16[512,256]{0,1:T(8,128)(2,1)S(1)}, u32[]{:S(2)}) copy-start(bf16[512,256]{0,1:T(8,128)(2,1)S(1)} %get-tuple-element.73) | copy-start | bytes 786436
  582.6 14.7 %copy-start.29 = (bf16[1024,4,64]{0,2,1:T(8,128)(2,1)S(1)}, bf16[1024,4,64]{0,2,1:T(8,128)(2,1)}, u32[]{:S(2)}) copy-start(bf16[1024,4,64]{0,2,1:T(8,128)(2,1)} %copy-done.28) | copy-start | bytes 1572868
  604.0 42.6 %copy-start.21 = (f32[512,4,64]{0,2,1:T(8,128)}, f32[512,4,64]{0,2,1:T(8,128)S(1)}, u32[]{:S(2)}) copy-start(f32[512,4,64]{0,2,1:T(8,128)S(1)} %convolution_bitcast_fusion.3) | copy-start | bytes 1572868
  655.1 65.9 %reduce-scatter.25.cloned.1.call-start = ((), (), s32[]{:S(2)}) async-start(), calls=%async_computation.28 | async-start | bytes 2621440 | tf_op jit(solution)/shard_map/reduce_scatter | solution.py:240
  668.1 98.4 %reduce-scatter.17.cloned.1.call-start = ((), (), s32[]{:S(2)}) async-start(), calls=%async_computation.20 | async-start | bytes 2621440 | tf_op jit(solution)/shard_map/reduce_scatter | solution.py:175
  673.0 158.7 %reduce-scatter.41.cloned.1.call-start = ((), (), s32[]{:S(2)}) async-start(), calls=%async_computation.38 | async-start | bytes 3244032 | tf_op jit(solution)/shard_map/reduce_scatter | solution.py:259
  680.1 227.6 %reduce-scatter.39.cloned.1.call-start = ((), (), s32[]{:S(2)}) async-start(), calls=%async_computation.37 | async-start | bytes 3244032 | tf_op jit(solution)/shard_map/reduce_scatter | solution.py:258
  687.4 296.5 %reduce-scatter.37.cloned.1.call-start = ((), (), s32[]{:S(2)}) async-start(), calls=%async_computation.36 | async-start | bytes 3244032 | tf_op jit(solution)/shard_map/reduce_scatter | solution.py:257
  694.6 354.3 %reduce-scatter.33.cloned.1.call-start = ((), (), s32[]{:S(2)}) async-start(), calls=%async_computation.34 | async-start | bytes 294912 | tf_op jit(solution)/shard_map/reduce_scatter | solution.py:255
  699.0 417.0 %reduce-scatter.35.cloned.1.call-start = ((), (), s32[]{:S(2)}) async-start(), calls=%async_computation.35 | async-start | bytes 1179648 | tf_op jit(solution)/shard_map/reduce_scatter | solution.py:256
  703.5 479.5 %reduce-scatter.31.cloned.1.call-start = ((), (), s32[]{:S(2)}) async-start(), calls=%async_computation.33 | async-start | bytes 1179648 | tf_op jit(solution)/shard_map/reduce_scatter | solution.py:254
  706.3 14.7 %copy-start.66 = (f32[1024]{0:T(1024)S(1)}, f32[1024]{0:T(1024)}, u32[]{:S(2)}) copy-start(f32[1024]{0:T(1024)} %copy-done.65) | copy-start | bytes 12292
  706.3 14.7 %copy-start.76 = (f32[256]{0:T(256)S(1)}, f32[256]{0:T(256)}, u32[]{:S(2)}) copy-start(f32[256]{0:T(256)} %copy-done.75) | copy-start | bytes 3076
  706.3 14.7 %copy-start.78 = (f32[256]{0:T(256)S(1)}, f32[256]{0:T(256)}, u32[]{:S(2)}) copy-start(f32[256]{0:T(256)} %copy-done.77) | copy-start | bytes 3076
  708.1 55.5 %copy-start.15 = (bf16[256,1024]{1,0:T(8,128)(2,1)S(1)}, bf16[256,1024]{1,0:T(8,128)(2,1)}, u32[]{:S(2)}) copy-start(bf16[256,1024]{1,0:T(8,128)(2,1)} %reduce-scatter.19.cloned.1.call-done) | copy-start | bytes 1572868
  708.1 55.5 %copy-start.17 = (bf16[2,256,1024]{2,1,0:T(8,128)(2,1)S(1)}, bf16[2,256,1024]{2,1,0:T(8,128)(2,1)}, u32[]{:S(2)}) copy-start(bf16[2,256,1024]{2,1,0:T(8,128)(2,1)} %param.13) | copy-start | bytes 3145732
  708.1 55.5 %copy-start.74 = (f32[256]{0:T(256)S(1)}, f32[256]{0:T(256)}, u32[]{:S(2)}) copy-start(f32[256]{0:T(256)} %copy-done.73) | copy-start | bytes 3076
  708.1 55.5 %copy-start.85 = (f32[256]{0:T(256)S(1)}, f32[256]{0:T(256)}, u32[]{:S(2)}) copy-start(f32[256]{0:T(256)} %copy-done.84) | copy-start | bytes 3076
  708.2 58.3 %copy-start.13 = (bf16[256,1024]{1,0:T(8,128)(2,1)S(1)}, bf16[256,1024]{1,0:T(8,128)(2,1)}, u32[]{:S(2)}) copy-start(bf16[256,1024]{1,0:T(8,128)(2,1)} %reduce-scatter.15.cloned.1.call-done) | copy-start | bytes 1572868
  708.2 58.3 %copy-start.83 = (f32[256]{0:T(256)S(1)}, f32[256]{0:T(256)}, u32[]{:S(2)}) copy-start(f32[256]{0:T(256)} %copy-done.82) | copy-start | bytes 3076
  (80 other events, 305.3 us)
Sparse Core Ops, SparseCore 0:
  56.0 22.3 all-gather.21
  80.6 22.5 all-gather.11
  175.5 31.3 reduce-scatter.14
  210.0 31.4 reduce-scatter.18
  392.5 31.7 reduce-scatter.26
  449.1 31.3 reduce-scatter.22
  483.0 31.3 reduce-scatter.20
Sparse Core Ops, SparseCore 1:
  195.7 42.9 all-gather.17
  245.8 22.4 all-gather.23
  270.2 43.1 all-gather.15
  315.4 41.3 all-gather.19
  358.3 20.6 all-gather.29
  381.2 22.4 all-gather.13
  405.2 30.4 all-gather.25
  518.4 22.4 all-gather.31
  542.9 22.4 all-gather.27
  655.2 31.4 reduce-scatter.28
  689.6 31.4 reduce-scatter.24
  723.7 31.4 reduce-scatter.16
  759.2 72.4 reduce-scatter.40
  835.8 71.9 reduce-scatter.38
  911.9 71.9 reduce-scatter.36
  987.8 61.0 reduce-scatter.32
  1052.9 63.1 reduce-scatter.34
  1120.4 62.5 reduce-scatter.30
where the time goes:
time: 1200 us; the launch traced here: 1190 us
  waiting for transfers between devices  717 us (60%)
  matrix products  200 us (17%)
  blocking collectives  169 us (14%)
  other arithmetic  69.8 us (6%)
  between operations  20.6 us (2%)
  local copies, waits for them, and re-layouts  12.5 us (1%)
    unnamed x2, blocking collectives  81.5 us
    reduce_scatter x1, waiting for transfers between devices, local(): lax.psum_scatter(gate_total, 'dp', scatter_dimension=0, tiled=True)  76.1 us
    reduce_scatter x1, waiting for transfers between devices, local(): lax.psum_scatter(up_total, 'dp', scatter_dimension=0, tiled=True)  76.1 us
    reduce_scatter x1, waiting for transfers between devices, local(): lax.psum_scatter(out_total, 'dp', scatter_dimension=1, tiled=True)  67.2 us
    reduce_scatter x1, waiting for transfers between devices, local(): lax.psum_scatter(query_total, 'dp', scatter_dimension=0, tiled=True)  67 us
    reduce_scatter x1, waiting for transfers between devices, local(): lax.psum_scatter(kv_total, 'dp', scatter_dimension=0, tiled=True)  65 us
    reduce_scatter x1, waiting for transfers between devices, local(): lax.psum_scatter(down_total, 'dp', scatter_dimension=1, tiled=True)  59.8 us
    reduce_scatter x2, waiting for transfers between devices, local(): lax.psum_scatter(jnp.dot(mixed_low, out_full, preferred_element_type=jnp....  47.6 us
  transfers between devices with their start and end apart: 25, of which 19 were waited for; matrix products, arithmetic and copies ran while one was open for 13% of the time, Pallas kernels for 0%

commit v1 on v0

--- a/solution.py
+++ b/solution.py
@@ -5,6 +5,11 @@
 
 epsilon = 1e-06
 neg_large = -1e30
+
+
+def gather_over(array, axis, along):
+    stack = jnp.stack([array] * lax.axis_size(axis))
+    return jnp.concatenate(lax.all_to_all(stack, axis, 0, 0), axis=along)
 
 
 def rope_tables(length, head_size):
@@ -137,7 +142,7 @@
             lax.all_gather(w_out, "dp", axis=1, tiled=True),
             lax.all_gather(w_gate, "dp", axis=0, tiled=True),
             lax.all_gather(w_up, "dp", axis=0, tiled=True),
-            lax.all_gather(w_down, "dp", axis=1, tiled=True),
+            gather_over(w_down, "dp", 1),
         )
         query_full, kv_full, out_full, gate_full, up_full, down_full = weights_now
         tokens = hidden_in[micro_idx].astype(jnp.float32)

time: 1200 us -> 1210 us (level)
  blocking collectives: 169 us -> 209 us
  waiting for transfers between devices: 717 us -> 684 us
    all_to_all x0 -> x1, blocking collectives: none -> 40.4 us  [gather_over(): return jnp.concatenate(lax.all_to_all(stack, axis, 0, 0), axis=along)]
    reduce_scatter x2, waiting for transfers between devices: 26.2 us -> 0.04 us  [local(): lax.psum_scatter(normed_two_part.astype(jnp.bfloat16), 'tp', scatter_dime...]
  transfers between devices with their start and end apart: 25 -> 25, of which waited for: 19 -> 18; matrix products, arithmetic and copies ran while one was open for 13% -> 13% of each run, Pallas kernels for 0% -> 0%
where the time goes in v1:
time: 1210 us; the launch traced here: 1200 us
  waiting for transfers between devices  684 us (57%)
  blocking collectives  209 us (17%)
  matrix products  198 us (16%)
  other arithmetic  69.6 us (6%)
  between operations  20.6 us (2%)
  local copies, waits for them, and re-layouts  13 us (1%)
    unnamed x2, blocking collectives  81.5 us
    reduce_scatter x1, waiting for transfers between devices, local(): lax.psum_scatter(up_total, 'dp', scatter_dimension=0, tiled=True)  76 us
    reduce_scatter x1, waiting for transfers between devices, local(): lax.psum_scatter(gate_total, 'dp', scatter_dimension=0, tiled=True)  75.5 us
    reduce_scatter x1, waiting for transfers between devices, local(): lax.psum_scatter(out_total, 'dp', scatter_dimension=1, tiled=True)  67 us
    reduce_scatter x1, waiting for transfers between devices, local(): lax.psum_scatter(query_total, 'dp', scatter_dimension=0, tiled=True)  66.9 us
    reduce_scatter x1, waiting for transfers between devices, local(): lax.psum_scatter(kv_total, 'dp', scatter_dimension=0, tiled=True)  64.9 us
    reduce_scatter x1, waiting for transfers between devices, local(): lax.psum_scatter(down_total, 'dp', scatter_dimension=1, tiled=True)  59.8 us
    reduce_scatter x2, waiting for transfers between devices, local(): lax.psum_scatter(jnp.dot(mixed_low, out_full, preferred_element_type=jnp....  47.6 us
  transfers between devices with their start and end apart: 25, of which 18 were waited for; matrix products, arithmetic and copies ran while one was open for 13% of the time, Pallas kernels for 0%

profile of v1, /device:TPU:0, one launch (start us, length us, event | category | flops | bytes accessed | tf_op | source)
XLA Modules:
  0.0 1197.7 jit_solution(7135087157578745638)
XLA Ops:
  11.3 42.1 %all-reduce.5 = (f32[1024]{0:T(1024)S(1)}, f32[1024]{0:T(1024)S(1)}) all-reduce(f32[1024]{0:T(1024)S(1)} %dynamic-update-slice, f32[1024]{0:T(1024)S(1)} %dynamic-update-slice.1), channel_id=1, replica_groups=mesh['dp'=8,'tp'=4] {'dp','tp'}, use_global_device_ids=true, to_apply=%add | all-reduce | flops 2048 | bytes 16384
  53.4 2.5 fusion.62
  56.7 26.1 %all_gather.66 = bf16[1024,64]{0,1:T(8,128)(2,1)S(1)} all-gather(bf16[128,64]{0,1:T(8,128)(2,1)S(1)} %copy-done.84), channel_id=1, replica_groups=mesh['dp'=8,'tp'=4] {'dp'}, dimensions={0}, use_global_device_ids=true | all-gather | bytes 147456 | tf_op jit(solution)/shard_map/all_gather | solution.py:141
  83.0 33.3 %all_gather.67 = bf16[1024,256]{1,0:T(8,128)(2,1)} all-gather(bf16[128,256]{1,0:T(8,128)(2,1)S(1)} %copy-done.70), channel_id=1, replica_groups=mesh['dp'=8,'tp'=4] {'dp'}, dimensions={0}, use_global_device_ids=true | all-gather | bytes 589824 | tf_op jit(solution)/shard_map/all_gather | solution.py:140
  116.4 28.1 %all_gather.68 = bf16[256,1024]{1,0:T(8,128)(2,1)} all-gather(bf16[256,128]{1,0:T(8,128)(2,1)S(1)} %copy-done.71), channel_id=1, replica_groups=mesh['dp'=8,'tp'=4] {'dp'}, dimensions={1}, use_global_device_ids=true | all-gather | bytes 589824 | tf_op jit(solution)/shard_map/all_gather | solution.py:142
  144.9 3.2 fusion.164
  156.8 6.1 exponential_reduce_fusion.3
  165.1 5.0 exponential_reduce_fusion.2
  174.8 5.1 exponential_reduce_fusion.1
  182.5 5.5 convolution_convert_fusion.7
  192.9 13.0 %reduce-scatter.15.cloned.1.call-done = bf16[256,1024]{1,0:T(8,128)(2,1)} async-done(((bf16[1024,1024]{1,0:T(8,128)(2,1)}), bf16[256,1024]{1,0:T(8,128)(2,1)}) %reduce-scatter.15.cloned.1.call-update) | async-done | bytes 524304 | tf_op jit(solution)/shard_map/reduce_scatter | solution.py:166
  205.9 34.6 %reduce-scatter.19.cloned.1.call-done = bf16[256,1024]{1,0:T(8,128)(2,1)} async-done(((bf16[1024,1024]{1,0:T(8,128)(2,1)}), bf16[256,1024]{1,0:T(8,128)(2,1)}) %reduce-scatter.19.cloned.1.call-update) | async-done | bytes 524304 | tf_op jit(solution)/shard_map/reduce_scatter | solution.py:166
  242.2 2.6 multiply_convert_fusion.7
  254.6 12.7 %all-gather.22.cloned.1.call-done = bf16[1024,1024]{1,0:T(8,128)(2,1)} async-done(((bf16[256,1024]{1,0:T(8,128)(2,1)}), bf16[1024,1024]{1,0:T(8,128)(2,1)}) %all-gather.22.cloned.1.call-update) | async-done | bytes 2097168 | tf_op jit(solution)/shard_map/all_gather | solution.py:174
  267.3 5.2 fusion.170
  272.6 39.8 %all-gather.16.cloned.1.call-done = bf16[1024,704]{0,1:T(8,128)(2,1)} async-done(((bf16[128,704]{0,1:T(8,128)(2,1)}), bf16[1024,704]{0,1:T(8,128)(2,1)}) %all-gather.16.cloned.1.call-update) | async-done | bytes 1441808 | tf_op jit(solution)/shard_map/all_gather | solution.py:143
  312.4 5.3 fusion.169
  317.7 38.1 %all-gather.26.cloned.1.call-done = bf16[704,1024]{1,0:T(8,128)(2,1)} async-done(((bf16[704,128]{1,0:T(8,128)(2,1)}), bf16[704,1024]{1,0:T(8,128)(2,1)}) %all-gather.26.cloned.1.call-update) | async-done | bytes 1441808 | tf_op jit(solution)/shard_map/all_gather | solution.py:193
  355.8 22.3 %all-gather.30.cloned.1.call-done = bf16[1024,1024]{1,0:T(8,128)(2,1)} async-done(((bf16[256,1024]{1,0:T(8,128)(2,1)}), bf16[1024,1024]{1,0:T(8,128)(2,1)}) %all-gather.30.cloned.1.call-update) | async-done | bytes 2097168 | tf_op jit(solution)/shard_map/all_gather | solution.py:197
  378.1 7.7 multiply_convert_fusion
  388.2 3.2 add_convert_fusion.1
  391.7 11.1 all-gather.14.cloned.1.call-done
  402.8 5.4 fusion.167
  408.2 3.3 fusion.166
  411.5 23.1 %all-gather.24.cloned.1.call-done = bf16[1024,1024]{1,0:T(8,128)(2,1)} async-done(((bf16[256,1024]{1,0:T(8,128)(2,1)}), bf16[1024,1024]{1,0:T(8,128)(2,1)}) %all-gather.24.cloned.1.call-update) | async-done | bytes 2097168 | tf_op jit(solution)/shard_map/all_gather | solution.py:197
  434.6 7.7 multiply_convert_fusion.2
  444.7 3.2 add_convert_fusion.3
  448.2 40.4 %all_to_all.6 = bf16[8,704,128]{2,1,0:T(8,128)(2,1)S(1)} all-to-all(bf16[8,704,128]{2,1,0:T(8,128)(2,1)S(1)} %stack.14), channel_id=1, replica_groups=mesh['dp'=8,'tp'=4] {'dp'}, dimensions={0} | all-to-all | bytes 2883584 | tf_op jit(solution)/shard_map/all_to_all | solution.py:12
  489.7 3.2 convolution_convert_fusion.2
  493.2 2.7 fusion.60
  495.9 26.3 %reduce-scatter.21.cloned.1.call-done = bf16[256,1024]{1,0:T(8,128)(2,1)} async-done(((bf16[1024,1024]{1,0:T(8,128)(2,1)}), bf16[256,1024]{1,0:T(8,128)(2,1)}) %reduce-scatter.21.cloned.1.call-update) | async-done | bytes 524304 | tf_op jit(solution)/shard_map/reduce_scatter | solution.py:180
  522.2 3.8 fusion.158
  526.7 21.9 %all-gather.32.cloned.1.call-done = bf16[1024,1024]{1,0:T(8,128)(2,1)} async-done(((bf16[256,1024]{1,0:T(8,128)(2,1)}), bf16[1024,1024]{1,0:T(8,128)(2,1)}) %all-gather.32.cloned.1.call-update) | async-done | bytes 2097168 | tf_op jit(solution)/shard_map/all_gather | solution.py:220
  548.6 2.6 convolution_convert_fusion.4
  551.9 4.6 fusion.103
  556.5 2.7 convolution_bitcast_fusion.7
  559.2 13.9 %all-gather.28.cloned.1.call-done = bf16[1024,1024]{1,0:T(8,128)(2,1)} async-done(((bf16[256,1024]{1,0:T(8,128)(2,1)}), bf16[1024,1024]{1,0:T(8,128)(2,1)}) %all-gather.28.cloned.1.call-update) | async-done | bytes 2097168 | tf_op jit(solution)/shard_map/all_gather | solution.py:220
  576.3 14.1 %fusion.9 = (f32[4,512]{1,0:T(4,128)S(1)}, f32[4,512]{1,0:T(4,128)S(1)}, f32[1024,512,4]{1,0,2:T(8,128)}) fusion(f32[1024,512,4]{1,0,2:T(8,128)} %copy-done.1, f32[4,512]{1,0:T(4,128)S(1)} %log_add_fusion.3, pred[512,1024]{0,1:T(8,128)(4,1)S(1)} %iota_compare_fusion.1, f32[1024,512,4]{1,0,2:T(8,128)} %fusion.103, f32[4,512]{1,0:T(4,128)S(1)} %log_add_fusion.1, ...), kind=kOutput, calls=%fused_computation.17 | convolution fusion | flops 285208576 | bytes 34504704 | tf_op jit(solution)/shard_map/tha,ua->htu/dot_general | solution.py:85
  590.4 14.7 %fusion.11 = (bf16[4,512,1024]{1,2,0:T(8,128)(2,1)}, bf16[4,512,1024]{1,2,0:T(8,128)(2,1)S(1)}) fusion(f32[1024,512,4]{1,0,2:T(8,128)} %get-tuple-element.108, f32[1024,512,4]{1,0,2:T(8,128)} %copy-done.1, f32[4,512]{1,0:T(4,128)S(1)} %get-tuple-element.26, f32[4,512]{1,0:T(4,128)S(1)} %log_add_fusion.3, pred[512,1024]{0,1:T(8,128)(4,1)S(1)} %iota_compare_fusion.1, ...), kind=kLoop, calls=%fused_computation.19 | loop fusion | flops 20971520 | bytes 42500096 | tf_op jit(solution)/shard_map/convert_element_type | solution.py:89
  605.2 5.8 convolution_bitcast_fusion.9
  613.5 4.3 convolution_bitcast_fusion.1
  617.8 4.5 fusion.101
  622.3 8.8 fusion.6
  631.1 14.8 %fusion.8 = (bf16[4,512,1024]{1,2,0:T(8,128)(2,1)S(1)}, bf16[4,512,1024]{1,2,0:T(8,128)(2,1)}) fusion(f32[1024,512,4]{1,0,2:T(8,128)} %get-tuple-element.107, f32[1024,512,4]{1,0,2:T(8,128)} %copy-done, f32[4,512]{1,0:T(4,128)S(1)} %get-tuple-element.28, f32[4,512]{1,0:T(4,128)S(1)} %log_add_fusion.2, pred[512,1024]{0,1:T(8,128)(4,1)S(1)} %iota_compare_fusion, ...), kind=kLoop, calls=%fused_computation.14 | loop fusion | flops 20971520 | bytes 42500096 | tf_op jit(solution)/shard_map/convert_element_type | solution.py:89
  645.9 3.2 convolution_bitcast_fusion
  665.9 5.9 convolution_bitcast_fusion.11
  676.2 4.5 convolution_convert_fusion.3
  680.8 3.8 fusion.176
  684.6 3.2 convolution_add_fusion.2
  688.0 3.9 fusion.179
  691.9 3.3 convolution_add_fusion
  695.2 3.8 fusion.178
  699.0 3.3 convolution_add_fusion.1
  706.9 2.5 fusion.88
  711.6 2.5 fusion.175
  716.0 12.8 %reduce-scatter.25.cloned.1.call-done = bf16[256,1024]{1,0:T(8,128)(2,1)} async-done(((bf16[1024,1024]{1,0:T(8,128)(2,1)}), bf16[256,1024]{1,0:T(8,128)(2,1)}) %reduce-scatter.25.cloned.1.call-update) | async-done | bytes 524304 | tf_op jit(solution)/shard_map/reduce_scatter | solution.py:245
  730.7 39.5 %all-reduce.4 = (f32[1024]{0:T(1024)S(1)}, f32[1024]{0:T(1024)S(1)}) all-reduce(f32[1024]{0:T(1024)S(1)} %add.272, f32[1024]{0:T(1024)S(1)} %add.273), channel_id=10, replica_groups=mesh['dp'=8,'tp'=4] {'dp','tp'}, use_global_device_ids=true, to_apply=%region_35.36.clone | all-reduce | flops 2048 | bytes 16384
  771.4 2.9 fusion.50
  779.6 59.8 %reduce-scatter.41.cloned.1.call-done = f32[704,128]{1,0:T(8,128)} async-done(((f32[704,1024]{1,0:T(8,128)}), f32[704,128]{1,0:T(8,128)}) %reduce-scatter.41.cloned.1.call-update) | async-done | bytes 360464 | tf_op jit(solution)/shard_map/reduce_scatter | solution.py:264
  839.4 76.0 %reduce-scatter.39.cloned.1.call-done = f32[128,704]{0,1:T(8,128)} async-done(((f32[1024,704]{0,1:T(8,128)}), f32[128,704]{0,1:T(8,128)}) %reduce-scatter.39.cloned.1.call-update) | async-done | bytes 360464 | tf_op jit(solution)/shard_map/reduce_scatter | solution.py:263
  915.4 75.5 %reduce-scatter.37.cloned.1.call-done = f32[128,704]{0,1:T(8,128)} async-done(((f32[1024,704]{0,1:T(8,128)}), f32[128,704]{0,1:T(8,128)}) %reduce-scatter.37.cloned.1.call-update) | async-done | bytes 360464 | tf_op jit(solution)/shard_map/reduce_scatter | solution.py:262
  990.9 64.9 %reduce-scatter.33.cloned.1.call-done = f32[128,64]{0,1:T(8,128)} async-done(((f32[1024,64]{0,1:T(8,128)}), f32[128,64]{0,1:T(8,128)}) %reduce-scatter.33.cloned.1.call-update) | async-done | bytes 32784 | tf_op jit(solution)/shard_map/reduce_scatter | solution.py:260
  1055.8 67.0 %reduce-scatter.35.cloned.1.call-done = f32[256,128]{1,0:T(8,128)} async-done(((f32[256,1024]{1,0:T(8,128)}), f32[256,128]{1,0:T(8,128)}) %reduce-scatter.35.cloned.1.call-update) | async-done | bytes 131088 | tf_op jit(solution)/shard_map/reduce_scatter | solution.py:261
  1122.9 66.9 %reduce-scatter.31.cloned.1.call-done = f32[128,256]{1,0:T(8,128)} async-done(((f32[1024,256]{1,0:T(8,128)}), f32[128,256]{1,0:T(8,128)}) %reduce-scatter.31.cloned.1.call-update) | async-done | bytes 131088 | tf_op jit(solution)/shard_map/reduce_scatter | solution.py:259
  (386 shorter events, 87.5 us)
Async XLA Ops:
  8.0 48.7 %copy-start.84 = (bf16[128,64]{0,1:T(8,128)(2,1)S(1)}, bf16[128,64]{0,1:T(8,128)(2,1)}, u32[]{:S(2)}) copy-start(bf16[128,64]{0,1:T(8,128)(2,1)} %param.19) | copy-start | bytes 49156
  8.0 75.0 %copy-start.70 = (bf16[128,256]{1,0:T(8,128)(2,1)S(1)}, bf16[128,256]{1,0:T(8,128)(2,1)}, u32[]{:S(2)}) copy-start(bf16[128,256]{1,0:T(8,128)(2,1)} %param.18) | copy-start | bytes 196612
  8.0 108.3 %copy-start.71 = (bf16[256,128]{1,0:T(8,128)(2,1)S(1)}, bf16[256,128]{1,0:T(8,128)(2,1)}, u32[]{:S(2)}) copy-start(bf16[256,128]{1,0:T(8,128)(2,1)} %param.20) | copy-start | bytes 196612
  8.0 136.8 %all-gather.20.cloned.1.call-start = ((), (), s32[]{:S(2)}) async-start(), calls=%async_computation.21 | async-start | bytes 2621440 | tf_op jit(solution)/shard_map/all_gather | solution.py:156
  9.6 135.2 %copy-start.78 = (f32[256]{0:T(256)}, f32[256]{0:T(256)S(1)}, u32[]{:S(2)}) copy-start(f32[256]{0:T(256)S(1)} %get-tuple-element.110) | copy-start | bytes 3076
  9.6 135.2 %copy-start.80 = (f32[256]{0:T(256)}, f32[256]{0:T(256)S(1)}, u32[]{:S(2)}) copy-start(f32[256]{0:T(256)S(1)} %get-tuple-element.109) | copy-start | bytes 3076
  53.4 91.5 %copy-start.68 = (f32[1024]{0:T(1024)}, f32[1024]{0:T(1024)S(1)}, u32[]{:S(2)}) copy-start(f32[1024]{0:T(1024)S(1)} %get-tuple-element.40) | copy-start | bytes 12292
  55.9 92.2 %all-gather.12.cloned.1.call-start = ((), (), s32[]{:S(2)}) async-start(), calls=%async_computation.15 | async-start | bytes 2621440 | tf_op jit(solution)/shard_map/all_gather | solution.py:156
  56.6 149.3 %reduce-scatter.15.cloned.1.call-start = ((), (), s32[]{:S(2)}) async-start(), calls=%async_computation.16 | async-start | bytes 2621440 | tf_op jit(solution)/shard_map/reduce_scatter | solution.py:166
  82.8 67.7 %copy-start.33 = (bf16[1024,64]{0,1:T(8,128)(2,1)}, bf16[1024,64]{0,1:T(8,128)(2,1)S(1)}, u32[]{:S(2)}) copy-start(bf16[1024,64]{0,1:T(8,128)(2,1)S(1)} %all_gather.66) | copy-start | bytes 393220
  82.8 70.2 %copy-start.90 = (f32[16]{0:T(128)}, f32[16]{0:T(128)S(1)}, u32[]{:S(2)}) copy-start(f32[16]{0:T(128)S(1)} %multiply_power_fusion) | copy-start | bytes 196
  82.8 70.2 %copy-start.74 = (f32[1024]{0:T(1024)}, f32[1024]{0:T(1024)S(1)}, u32[]{:S(2)}) copy-start(f32[1024]{0:T(1024)S(1)} %iota_convert_fusion) | copy-start | bytes 12292
  150.5 19.6 %copy-start.38 = (bf16[1024,64]{0,1:T(8,128)(2,1)}, bf16[1024,64]{0,1:T(8,128)(2,1)S(1)}, u32[]{:S(2)}) copy-start(bf16[1024,64]{0,1:T(8,128)(2,1)S(1)} %get-tuple-element.97) | copy-start | bytes 393220
  153.4 11.7 copy-start.57
  153.4 11.7 copy-start.59
  155.2 15.0 %copy-start = (f32[1024,512,4]{1,0,2:T(8,128)}, f32[1024,512,4]{1,0,2:T(8,128)S(1)}, u32[]{:S(2)}) copy-start(f32[1024,512,4]{1,0,2:T(8,128)S(1)} %get-tuple-element.100) | copy-start | bytes 25165828
  170.2 460.9 %copy-start.64 = (f32[4,512]{1,0:T(4,128)}, f32[4,512]{1,0:T(4,128)S(1)}, u32[]{:S(2)}) copy-start(f32[4,512]{1,0:T(4,128)S(1)} %log_add_fusion.2) | copy-start | bytes 24580
  174.5 66.1 %reduce-scatter.19.cloned.1.call-start = ((), (), s32[]{:S(2)}) async-start(), calls=%async_computation.22 | async-start | bytes 2621440 | tf_op jit(solution)/shard_map/reduce_scatter | solution.py:166
  182.4 448.7 %copy-start.66 = (f32[4,512]{1,0:T(4,128)}, f32[4,512]{1,0:T(4,128)S(1)}, u32[]{:S(2)}) copy-start(f32[4,512]{1,0:T(4,128)S(1)} %log_add_fusion) | copy-start | bytes 24580
  190.2 50.4 %copy-start.3 = (bf16[2,256,1024]{2,1,0:T(8,128)(2,1)S(1)}, bf16[2,256,1024]{2,1,0:T(8,128)(2,1)}, u32[]{:S(2)}) copy-start(bf16[2,256,1024]{2,1,0:T(8,128)(2,1)} %param.12) | copy-start | bytes 3145732
  192.3 62.3 %all-gather.18.cloned.1.call-start = ((), (), s32[]{:S(2)}) async-start(), calls=%async_computation.19 | async-start | bytes 1622016 | tf_op jit(solution)/shard_map/all_gather | solution.py:144
  192.8 53.3 %copy-start.89 = (s32[16]{0:T(128)S(1)}, s32[16]{0:T(128)}, u32[]{:S(2)}) copy-start(s32[16]{0:T(128)} %param.14) | copy-start | bytes 196
  192.9 54.0 %copy-start.92 = (f32[8]{0:T(128)S(1)}, f32[8]{0:T(128)}, u32[]{:S(2)}) copy-start(f32[8]{0:T(128)} %param.15) | copy-start | bytes 100
  192.9 58.6 %copy-start.16 = (bf16[2,256,1024]{2,1,0:T(8,128)(2,1)S(1)}, bf16[2,256,1024]{2,1,0:T(8,128)(2,1)}, u32[]{:S(2)}) copy-start(bf16[2,256,1024]{2,1,0:T(8,128)(2,1)} %param.13) | copy-start | bytes 3145732
  192.9 74.4 %all-gather.22.cloned.1.call-start = ((), (), s32[]{:S(2)}) async-start(), calls=%async_computation.23 | async-start | bytes 2621440 | tf_op jit(solution)/shard_map/all_gather | solution.py:174
  242.2 280.1 %copy-start.76 = (f32[256]{0:T(256)}, f32[256]{0:T(256)S(1)}, u32[]{:S(2)}) copy-start(f32[256]{0:T(256)S(1)} %add_rsqrt_fusion) | copy-start | bytes 3076
  244.8 67.6 %all-gather.16.cloned.1.call-start = ((), (), s32[]{:S(2)}) async-start(), calls=%async_computation.18 | async-start | bytes 1622016 | tf_op jit(solution)/shard_map/all_gather | solution.py:143
  245.3 110.5 %all-gather.26.cloned.1.call-start = ((), (), s32[]{:S(2)}) async-start(), calls=%async_computation.26 | async-start | bytes 1622016 | tf_op jit(solution)/shard_map/all_gather | solution.py:193
  246.1 132.0 %all-gather.30.cloned.1.call-start = ((), (), s32[]{:S(2)}) async-start(), calls=%async_computation.30 | async-start | bytes 2621440 | tf_op jit(solution)/shard_map/all_gather | solution.py:197
  252.7 150.0 %all-gather.14.cloned.1.call-start = ((), (), s32[]{:S(2)}) async-start(), calls=%async_computation.17 | async-start | bytes 2621440 | tf_op jit(solution)/shard_map/all_gather | solution.py:174
  253.4 181.2 %all-gather.24.cloned.1.call-start = ((), (), s32[]{:S(2)}) async-start(), calls=%async_computation.25 | async-start | bytes 2621440 | tf_op jit(solution)/shard_map/all_gather | solution.py:197
  254.0 239.2 %reduce-scatter.27.cloned.1.call-start = ((), (), s32[]{:S(2)}) async-start(), calls=%async_computation.31 | async-start | bytes 2621440 | tf_op jit(solution)/shard_map/reduce_scatter | solution.py:215
  391.4 101.8 %reduce-scatter.23.cloned.1.call-start = ((), (), s32[]{:S(2)}) async-start(), calls=%async_computation.27 | async-start | bytes 2621440 | tf_op jit(solution)/shard_map/reduce_scatter | solution.py:215
  447.9 74.3 %reduce-scatter.21.cloned.1.call-start = ((), (), s32[]{:S(2)}) async-start(), calls=%async_computation.24 | async-start | bytes 2621440 | tf_op jit(solution)/shard_map/reduce_scatter | solution.py:180
  448.0 41.7 %copy-start.105 = (bf16[1024,704]{0,1:T(8,128)(2,1)S(1)}, bf16[1024,704]{0,1:T(8,128)(2,1)}, u32[]{:S(2)}) copy-start(bf16[1024,704]{0,1:T(8,128)(2,1)} %get-tuple-element.50) | copy-start | bytes 4325380
  492.9 55.7 %all-gather.32.cloned.1.call-start = ((), (), s32[]{:S(2)}) async-start(), calls=%async_computation.32 | async-start | bytes 2621440 | tf_op jit(solution)/shard_map/all_gather | solution.py:220
  495.9 30.1 %copy-start.85 = (f32[256]{0:T(256)}, f32[256]{0:T(256)S(1)}, u32[]{:S(2)}) copy-start(f32[256]{0:T(256)S(1)} %broadcast_multiply_fusion.3) | copy-start | bytes 3076
  495.9 30.1 %copy-start.87 = (f32[256]{0:T(256)}, f32[256]{0:T(256)S(1)}, u32[]{:S(2)}) copy-start(f32[256]{0:T(256)S(1)} %broadcast_multiply_fusion.1) | copy-start | bytes 3076
  526.1 47.1 %all-gather.28.cloned.1.call-start = ((), (), s32[]{:S(2)}) async-start(), calls=%async_computation.28 | async-start | bytes 2621440 | tf_op jit(solution)/shard_map/all_gather | solution.py:220
  526.6 189.3 %reduce-scatter.29.cloned.1.call-start = ((), (), s32[]{:S(2)}) async-start(), calls=%async_computation.33 | async-start | bytes 2621440 | tf_op jit(solution)/shard_map/reduce_scatter | solution.py:245
  556.5 16.7 %copy-start.25 = (bf16[256,1024]{1,0:T(8,128)(2,1)S(1)}, bf16[256,1024]{1,0:T(8,128)(2,1)}, u32[]{:S(2)}) copy-start(bf16[256,1024]{1,0:T(8,128)(2,1)} %all_gather.68) | copy-start | bytes 1572868
  559.2 17.0 %copy-start.39 = (bf16[1024,64]{0,1:T(8,128)(2,1)S(1)}, bf16[1024,64]{0,1:T(8,128)(2,1)}, u32[]{:S(2)}) copy-start(bf16[1024,64]{0,1:T(8,128)(2,1)} %copy-done.38) | copy-start | bytes 393220
  576.3 14.1 %copy-start.46 = (bf16[512,256]{0,1:T(8,128)(2,1)}, bf16[512,256]{0,1:T(8,128)(2,1)S(1)}, u32[]{:S(2)}) copy-start(bf16[512,256]{0,1:T(8,128)(2,1)S(1)} %get-tuple-element.73) | copy-start | bytes 786436
  590.4 14.8 %copy-start.29 = (bf16[1024,4,64]{0,2,1:T(8,128)(2,1)S(1)}, bf16[1024,4,64]{0,2,1:T(8,128)(2,1)}, u32[]{:S(2)}) copy-start(bf16[1024,4,64]{0,2,1:T(8,128)(2,1)} %copy-done.28) | copy-start | bytes 1572868
  611.0 11.3 slice-start.4
  611.8 42.6 %copy-start.21 = (f32[512,4,64]{0,2,1:T(8,128)}, f32[512,4,64]{0,2,1:T(8,128)S(1)}, u32[]{:S(2)}) copy-start(f32[512,4,64]{0,2,1:T(8,128)S(1)} %convolution_bitcast_fusion.3) | copy-start | bytes 1572868
  612.0 10.2 slice-start
  662.9 65.9 %reduce-scatter.25.cloned.1.call-start = ((), (), s32[]{:S(2)}) async-start(), calls=%async_computation.29 | async-start | bytes 2621440 | tf_op jit(solution)/shard_map/reduce_scatter | solution.py:245
  675.9 98.3 %reduce-scatter.17.cloned.1.call-start = ((), (), s32[]{:S(2)}) async-start(), calls=%async_computation.20 | async-start | bytes 2621440 | tf_op jit(solution)/shard_map/reduce_scatter | solution.py:180
  680.7 158.7 %reduce-scatter.41.cloned.1.call-start = ((), (), s32[]{:S(2)}) async-start(), calls=%async_computation.39 | async-start | bytes 3244032 | tf_op jit(solution)/shard_map/reduce_scatter | solution.py:264
  687.9 227.5 %reduce-scatter.39.cloned.1.call-start = ((), (), s32[]{:S(2)}) async-start(), calls=%async_computation.38 | async-start | bytes 3244032 | tf_op jit(solution)/shard_map/reduce_scatter | solution.py:263
  695.2 295.8 %reduce-scatter.37.cloned.1.call-start = ((), (), s32[]{:S(2)}) async-start(), calls=%async_computation.37 | async-start | bytes 3244032 | tf_op jit(solution)/shard_map/reduce_scatter | solution.py:262
  702.4 353.5 %reduce-scatter.33.cloned.1.call-start = ((), (), s32[]{:S(2)}) async-start(), calls=%async_computation.35 | async-start | bytes 294912 | tf_op jit(solution)/shard_map/reduce_scatter | solution.py:260
  706.8 416.1 %reduce-scatter.35.cloned.1.call-start = ((), (), s32[]{:S(2)}) async-start(), calls=%async_computation.36 | async-start | bytes 1179648 | tf_op jit(solution)/shard_map/reduce_scatter | solution.py:261
  711.2 478.6 %reduce-scatter.31.cloned.1.call-start = ((), (), s32[]{:S(2)}) async-start(), calls=%async_computation.34 | async-start | bytes 1179648 | tf_op jit(solution)/shard_map/reduce_scatter | solution.py:259
  714.1 14.7 %copy-start.69 = (f32[1024]{0:T(1024)S(1)}, f32[1024]{0:T(1024)}, u32[]{:S(2)}) copy-start(f32[1024]{0:T(1024)} %copy-done.68) | copy-start | bytes 12292
  714.1 14.7 %copy-start.79 = (f32[256]{0:T(256)S(1)}, f32[256]{0:T(256)}, u32[]{:S(2)}) copy-start(f32[256]{0:T(256)} %copy-done.78) | copy-start | bytes 3076
  714.1 14.7 %copy-start.81 = (f32[256]{0:T(256)S(1)}, f32[256]{0:T(256)}, u32[]{:S(2)}) copy-start(f32[256]{0:T(256)} %copy-done.80) | copy-start | bytes 3076
  715.9 55.5 %copy-start.15 = (bf16[256,1024]{1,0:T(8,128)(2,1)S(1)}, bf16[256,1024]{1,0:T(8,128)(2,1)}, u32[]{:S(2)}) copy-start(bf16[256,1024]{1,0:T(8,128)(2,1)} %reduce-scatter.19.cloned.1.call-done) | copy-start | bytes 1572868
  715.9 55.5 %copy-start.17 = (bf16[2,256,1024]{2,1,0:T(8,128)(2,1)S(1)}, bf16[2,256,1024]{2,1,0:T(8,128)(2,1)}, u32[]{:S(2)}) copy-start(bf16[2,256,1024]{2,1,0:T(8,128)(2,1)} %param.13) | copy-start | bytes 3145732
  715.9 55.5 %copy-start.77 = (f32[256]{0:T(256)S(1)}, f32[256]{0:T(256)}, u32[]{:S(2)}) copy-start(f32[256]{0:T(256)} %copy-done.76) | copy-start | bytes 3076
  715.9 55.5 %copy-start.88 = (f32[256]{0:T(256)S(1)}, f32[256]{0:T(256)}, u32[]{:S(2)}) copy-start(f32[256]{0:T(256)} %copy-done.87) | copy-start | bytes 3076
  715.9 58.3 %copy-start.13 = (bf16[256,1024]{1,0:T(8,128)(2,1)S(1)}, bf16[256,1024]{1,0:T(8,128)(2,1)}, u32[]{:S(2)}) copy-start(bf16[256,1024]{1,0:T(8,128)(2,1)} %reduce-scatter.15.cloned.1.call-done) | copy-start | bytes 1572868
  716.0 58.3 %copy-start.86 = (f32[256]{0:T(256)S(1)}, f32[256]{0:T(256)}, u32[]{:S(2)}) copy-start(f32[256]{0:T(256)} %copy-done.85) | copy-start | bytes 3076
  (83 other events, 309.5 us)
Sparse Core Ops, SparseCore 0:
  56.0 22.3 all-gather.19
  80.6 22.5 all-gather.11
  174.6 31.3 reduce-scatter.14
  209.1 31.4 reduce-scatter.18
  391.6 31.6 reduce-scatter.26
  448.1 31.4 reduce-scatter.22
  493.0 29.1 reduce-scatter.20
Sparse Core Ops, SparseCore 1:
  194.8 42.9 all-gather.17
  244.8 22.4 all-gather.21
  269.2 43.1 all-gather.15
  314.5 41.3 all-gather.25
  357.4 20.6 all-gather.29
  380.3 22.4 all-gather.13
  404.3 30.3 all-gather.23
  526.2 22.4 all-gather.31
  550.7 22.4 all-gather.27
  663.0 31.4 reduce-scatter.28
  697.4 31.3 reduce-scatter.24
  731.5 31.5 reduce-scatter.16
  767.0 72.3 reduce-scatter.40
  843.5 71.8 reduce-scatter.38
  919.6 71.3 reduce-scatter.36
  994.8 61.0 reduce-scatter.32
  1059.8 63.0 reduce-scatter.34
  1127.3 62.5 reduce-scatter.30
